TPU v7x, 32 devices: a whole 2x2x4 slice. The times are simulated.
32 devices in a mesh: dp: 8 (over z, x), tensor: 4 (over y, core).
Axes of the slice: x: 2, y: 2, z: 4, core: 2. Of those that a mesh axis runs over, the one named last changes fastest.
Arguments:
- tokens: bfloat16 [16384, 768], P('dp'), may hold values from -6 to 6
- seq_lengths: int32 [8, 9], P('dp'), may hold values from 1 to 512, 2048 in all within a row
- query_weight: bfloat16 [768, 768], P(None, 'tensor'), may hold values from -0.21875 to 0.21875
- key_weight: bfloat16 [768, 768], P(None, 'tensor'), may hold values from -0.21875 to 0.21875
- value_weight: bfloat16 [768, 768], P(None, 'tensor'), may hold values from -0.21875 to 0.21875
- out_weight: bfloat16 [768, 768], P('tensor'), may hold values from -0.875 to 0.875
- ffn_in: bfloat16 [768, 3072], P(None, 'tensor'), may hold values from -0.21875 to 0.21875
- ffn_out: bfloat16 [3072, 768], P('tensor'), may hold values from -0.109375 to 0.109375
- gain_attn: float32 [768], replicated, may hold values from 0.5 to 1.5
- gain_ffn: float32 [768], replicated, may hold values from 0.5 to 1.5
- query_down: bfloat16 [768, 8], replicated, may hold values from -0.21875 to 0.21875
- value_down: bfloat16 [768, 8], replicated, may hold values from -0.21875 to 0.21875
- query_up: bfloat16 [8, 12, 64], P(None, 'tensor'), may hold values from -1.078125 to 1.078125
- value_up: bfloat16 [8, 12, 64], P(None, 'tensor'), may hold values from -1.078125 to 1.078125
- cotangent: bfloat16 [16384, 768], P('dp'), may hold values from -6 to 6
Outputs:
- activations: bfloat16 [16384, 768], P(('dp', 'tensor'))
- input_grad: float32 [16384, 768], P(('dp', 'tensor'))
- query_up_grad: float32 [8, 12, 64], P(None, 'tensor', 'dp')
- value_up_grad: float32 [8, 12, 64], P(None, 'tensor', 'dp')
Inputs may be any that keep to these rules, and one draw needn't show every extreme that they name: `seq_lengths`: row b holds the lengths of the 8 sequences packed from the start of the b-th block of 2048 slots, in order, then the number of padding slots at the block's end; every row sums to 2048 and reaches 512.
All inputs are finite; a program needn't handle non-finite values.
Results may differ from a plain program's by a relative error of at most 0.025.
Values may be sent and summed in bfloat16 or wider, within the bound.
A program may use at most 128 MiB of HBM per device.

v0:
```python
import jax
import jax.numpy as jnp
from jax import lax
from jax.sharding import PartitionSpec as P

H = 12
HD = 64
R = 8
SEQ = 512
EPSILON = 1e-05
NEGATIVE = -1e30


def normalize(vector, scale_gain):
    average = jnp.mean(vector, axis=-1, keepdims=True)
    centered = vector - average
    inverse = lax.rsqrt(jnp.mean(centered * centered, axis=-1, keepdims=True) + EPSILON)
    unit_rows = centered * inverse
    return (unit_rows * scale_gain, unit_rows, inverse)


def normalize_back(upstream, unit_rows, inverse, scale_gain):
    scaled = upstream * scale_gain
    return inverse * (
        scaled
        - jnp.mean(scaled, axis=-1, keepdims=True)
        - unit_rows * jnp.mean(scaled * unit_rows, axis=-1, keepdims=True)
    )


def segment_ids(seg_ends, positions, block_rows):
    counted = jnp.sum((positions[:, None] >= seg_ends[None, :]).astype(jnp.int32), axis=1)
    inside = (positions >= 0) & (positions < block_rows)
    segment = jnp.where(inside, counted, -2)
    is_valid = inside & (counted < seg_ends.shape[0] - 1)
    return (segment, is_valid)


def transpose_dot(left_side, right_side):
    return lax.dot_general(
        left_side, right_side, (((1,), (1,)), ((), ())), preferred_element_type=jnp.float32
    )


def block_scores(
    block_index,
    queries,
    keys_ext,
    values_ext,
    seg_query,
    seg_keys,
    valid_query,
    head_count,
    block_span,
):
    col_width = queries.shape[1]
    head_size = col_width // head_count
    row_start = block_index * block_span
    query_block = lax.dynamic_slice_in_dim(queries, row_start, block_span, 0).reshape(
        block_span, head_count, head_size
    )
    key_block = lax.dynamic_slice_in_dim(keys_ext, row_start, 3 * block_span, 0).reshape(
        3 * block_span, head_count, head_size
    )
    value_block = lax.dynamic_slice_in_dim(values_ext, row_start, 3 * block_span, 0).reshape(
        3 * block_span, head_count, head_size
    )
    seg_rows = lax.dynamic_slice_in_dim(seg_query, row_start, block_span, 0)
    seg_cols = lax.dynamic_slice_in_dim(seg_keys, row_start, 3 * block_span, 0)
    valid_rows = lax.dynamic_slice_in_dim(valid_query, row_start, block_span, 0)
    allowed = (seg_rows[:, None] == seg_cols[None, :]) & valid_rows[:, None]
    scores = jnp.einsum(
        "qhd,khd->hqk", query_block, key_block, preferred_element_type=jnp.float32
    ) * head_size ** (-0.5)
    masked = jnp.where(allowed[None], scores, NEGATIVE)
    return (query_block, key_block, value_block, allowed, masked, valid_rows)


def attend_forward(
    block_index,
    queries,
    keys_ext,
    values_ext,
    seg_query,
    seg_keys,
    valid_query,
    head_count,
    block_span,
):
    query_block, key_block, value_block, allowed, masked, valid_rows = block_scores(
        block_index,
        queries,
        keys_ext,
        values_ext,
        seg_query,
        seg_keys,
        valid_query,
        head_count,
        block_span,
    )
    row_max = jnp.max(masked, axis=-1, keepdims=True)
    weights = jnp.where(allowed[None], jnp.exp(masked - row_max), 0.0)
    row_total = (
        jnp.sum(weights, axis=-1, keepdims=True)
        + (1.0 - valid_rows.astype(jnp.float32))[None, :, None]
    )
    probability = (weights / row_total).astype(jnp.bfloat16)
    mixed_rows = jnp.einsum(
        "hqk,khd->qhd", probability, value_block, preferred_element_type=jnp.float32
    )
    return (
        mixed_rows.reshape(block_span, queries.shape[1]),
        (row_max + jnp.log(row_total))[:, :, 0],
    )


def attend_backward(
    block_index,
    queries,
    keys_ext,
    values_ext,
    seg_query,
    seg_keys,
    valid_query,
    head_count,
    block_span,
    log_total,
    grad_context,
):
    query_block, key_block, value_block, allowed, masked, valid_rows = block_scores(
        block_index,
        queries,
        keys_ext,
        values_ext,
        seg_query,
        seg_keys,
        valid_query,
        head_count,
        block_span,
    )
    col_width = queries.shape[1]
    head_size = col_width // head_count
    score_scale = head_size ** (-0.5)
    stored = log_total[block_index]
    probability = jnp.where(allowed[None], jnp.exp(masked - stored[:, :, None]), 0.0)
    grad_block = lax.dynamic_slice_in_dim(
        grad_context, block_index * block_span, block_span, 0
    ).reshape(block_span, head_count, head_size)
    grad_prob = jnp.einsum(
        "qhd,khd->hqk", grad_block, value_block, preferred_element_type=jnp.float32
    )
    row_delta = jnp.sum(probability * grad_prob, axis=-1, keepdims=True)
    grad_scores = (probability * (grad_prob - row_delta)).astype(jnp.bfloat16)
    grad_query = (
        jnp.einsum("hqk,khd->qhd", grad_scores, key_block, preferred_element_type=jnp.float32)
        * score_scale
    )
    grad_key = (
        jnp.einsum("hqk,qhd->khd", grad_scores, query_block, preferred_element_type=jnp.float32)
        * score_scale
    )
    grad_value = jnp.einsum(
        "hqk,qhd->khd",
        probability.astype(jnp.bfloat16),
        grad_block,
        preferred_element_type=jnp.float32,
    )
    return (
        grad_query.reshape(block_span, col_width),
        grad_key.reshape(3 * block_span, col_width),
        grad_value.reshape(3 * block_span, col_width),
    )


def on_device(
    tokens,
    seq_lengths,
    query_weight,
    key_weight,
    value_weight,
    out_weight,
    ffn_in,
    ffn_out,
    gain_attn,
    gain_ffn,
    query_down,
    value_down,
    query_up,
    value_up,
    cotangent,
):
    groups = lax.axis_size("tensor")
    member = lax.axis_index("tensor")
    block_span = SEQ
    block_rows = tokens.shape[0]
    own_rows = block_rows // groups
    seg_ends = jnp.cumsum(seq_lengths[0])
    w_query, w_key, w_value, w_inner, w_out, w_ffn_out, up_query, up_value = (
        query_weight,
        key_weight,
        value_weight,
        ffn_in,
        out_weight,
        ffn_out,
        query_up,
        value_up,
    )
    first_row = 0
    head_count = H // groups
    row_count = tokens.shape[0]
    col_width = w_query.shape[1]
    up_query_flat = up_query.reshape(R, col_width)
    up_value_flat = up_value.reshape(R, col_width)
    down_query_wide = query_down.astype(jnp.float32)
    down_value_wide = value_down.astype(jnp.float32)
    low_query = jnp.dot(tokens, query_down, preferred_element_type=jnp.float32).astype(jnp.bfloat16)
    low_value = jnp.dot(tokens, value_down, preferred_element_type=jnp.float32).astype(jnp.bfloat16)
    queries = (
        jnp.dot(tokens, w_query, preferred_element_type=jnp.float32)
        + 2.0 * jnp.dot(low_query, up_query_flat, preferred_element_type=jnp.float32)
    ).astype(jnp.bfloat16)
    key_rows = jnp.dot(tokens, w_key, preferred_element_type=jnp.float32).astype(jnp.bfloat16)
    values = (
        jnp.dot(tokens, w_value, preferred_element_type=jnp.float32)
        + 2.0 * jnp.dot(low_value, up_value_flat, preferred_element_type=jnp.float32)
    ).astype(jnp.bfloat16)
    key_value = jnp.stack([key_rows, values])
    key_value_ext = jnp.pad(key_value, ((0, 0), (block_span, block_span), (0, 0)))
    keys_ext = key_value_ext[0]
    values_ext = key_value_ext[1]
    positions = first_row - block_span + jnp.arange(row_count + 2 * block_span, dtype=jnp.int32)
    seg_keys, valid_keys = segment_ids(seg_ends, positions, block_rows)
    seg_query = seg_keys[block_span : block_span + row_count]
    valid_query = valid_keys[block_span : block_span + row_count]
    valid_rows = valid_query.astype(jnp.float32)[:, None]
    block_count = row_count // block_span

    def forward_block(block_index):
        return attend_forward(
            block_index,
            queries,
            keys_ext,
            values_ext,
            seg_query,
            seg_keys,
            valid_query,
            head_count,
            block_span,
        )

    context_blocks, log_total = lax.map(forward_block, jnp.arange(block_count))
    context = context_blocks.reshape(row_count, col_width).astype(jnp.bfloat16)
    attn_out = lax.psum(
        jnp.dot(context, w_out, preferred_element_type=jnp.float32).astype(jnp.bfloat16), "tensor"
    ).astype(jnp.float32)
    normed, unit_one, inverse_one = normalize(tokens.astype(jnp.float32) + attn_out, gain_attn)
    normed_low = normed.astype(jnp.bfloat16)
    pre_act = jnp.dot(normed_low, w_inner, preferred_element_type=jnp.float32)
    active = jax.nn.gelu(pre_act, approximate=False).astype(jnp.bfloat16)
    ffn_result = lax.psum(
        jnp.dot(active, w_ffn_out, preferred_element_type=jnp.float32).astype(jnp.bfloat16),
        "tensor",
    ).astype(jnp.float32)
    final_rows, unit_two, inverse_two = normalize(normed + ffn_result, gain_ffn)
    final_rows = final_rows * valid_rows
    grad_final = cotangent.astype(jnp.float32) * valid_rows
    grad_mid = normalize_back(grad_final, unit_two, inverse_two, gain_ffn)
    grad_active = transpose_dot(grad_mid.astype(jnp.bfloat16), w_ffn_out)
    recomputed = jnp.dot(
        lax.optimization_barrier(normed_low), w_inner, preferred_element_type=jnp.float32
    )
    gelu_pull = jax.vjp(lambda argument: jax.nn.gelu(argument, approximate=False), recomputed)[1]
    grad_pre = gelu_pull(grad_active)[0].astype(jnp.bfloat16)
    grad_normed = grad_mid + lax.psum(
        transpose_dot(grad_pre, w_inner).astype(jnp.bfloat16), "tensor"
    ).astype(jnp.float32)
    grad_mixed = normalize_back(grad_normed, unit_one, inverse_one, gain_attn)
    grad_context = transpose_dot(grad_mixed.astype(jnp.bfloat16), w_out).astype(jnp.bfloat16)

    def back_step(accumulated, block_index):
        key_total, value_total = accumulated
        grad_query, grad_key, grad_value = attend_backward(
            block_index,
            queries,
            keys_ext,
            values_ext,
            seg_query,
            seg_keys,
            valid_query,
            head_count,
            block_span,
            log_total,
            grad_context,
        )
        row_start = block_index * block_span
        key_total = lax.dynamic_update_slice_in_dim(
            key_total,
            lax.dynamic_slice_in_dim(key_total, row_start, 3 * block_span, 0) + grad_key,
            row_start,
            0,
        )
        value_total = lax.dynamic_update_slice_in_dim(
            value_total,
            lax.dynamic_slice_in_dim(value_total, row_start, 3 * block_span, 0) + grad_value,
            row_start,
            0,
        )
        return ((key_total, value_total), grad_query)

    empty_ext = jnp.zeros((row_count + 2 * block_span, col_width), jnp.float32)
    (key_total, value_total), query_grads = lax.scan(
        back_step, (empty_ext, empty_ext), jnp.arange(block_count)
    )
    key_middle = key_total[block_span : block_span + row_count]
    value_middle = value_total[block_span : block_span + row_count]
    grad_queries = query_grads.reshape(row_count, col_width).astype(jnp.bfloat16)
    grad_keys = key_middle.astype(jnp.bfloat16)
    grad_values = value_middle.astype(jnp.bfloat16)
    input_term = (
        transpose_dot(grad_queries, w_query)
        + transpose_dot(grad_keys, w_key)
        + transpose_dot(grad_values, w_value)
    )
    low_query_grad = 2.0 * transpose_dot(grad_queries, up_query_flat)
    low_value_grad = 2.0 * transpose_dot(grad_values, up_value_flat)
    input_term = input_term + jnp.dot(
        low_query_grad,
        down_query_wide.T,
        precision=lax.Precision.HIGHEST,
        preferred_element_type=jnp.float32,
    )
    input_term = input_term + jnp.dot(
        low_value_grad,
        down_value_wide.T,
        precision=lax.Precision.HIGHEST,
        preferred_element_type=jnp.float32,
    )
    grad_input = grad_mixed + lax.psum(input_term.astype(jnp.bfloat16), "tensor").astype(
        jnp.float32
    )
    adapter_query = (
        2.0
        * lax.dot_general(
            low_query, grad_queries, (((0,), (0,)), ((), ())), preferred_element_type=jnp.float32
        )
    ).reshape(R, head_count, HD)
    adapter_value = (
        2.0
        * lax.dot_general(
            low_value, grad_values, (((0,), (0,)), ((), ())), preferred_element_type=jnp.float32
        )
    ).reshape(R, head_count, HD)
    grad_up_query, grad_up_value = (
        lax.psum_scatter(adapter_query, "dp", scatter_dimension=2, tiled=True),
        lax.psum_scatter(adapter_value, "dp", scatter_dimension=2, tiled=True),
    )
    out_rows = lax.dynamic_slice_in_dim(final_rows, member * own_rows, own_rows, 0).astype(
        jnp.bfloat16
    )
    out_grads = lax.dynamic_slice_in_dim(grad_input, member * own_rows, own_rows, 0)
    return (out_rows, out_grads, grad_up_query, grad_up_value)


def solution(mesh):
    in_specs = (
        P("dp", None),
        P("dp", None),
        P(None, "tensor"),
        P(None, "tensor"),
        P(None, "tensor"),
        P("tensor", None),
        P(None, "tensor"),
        P("tensor", None),
        P(),
        P(),
        P(),
        P(),
        P(None, "tensor", None),
        P(None, "tensor", None),
        P("dp", None),
    )
    out_specs = (
        P(("dp", "tensor"), None),
        P(("dp", "tensor"), None),
        P(None, "tensor", "dp"),
        P(None, "tensor", "dp"),
    )
    return jax.shard_map(
        on_device, mesh=mesh, in_specs=in_specs, out_specs=out_specs, check_vma=False
    )
```

profile of v0, /device:TPU:0, one launch (start us, length us, event | category | flops | bytes accessed | tf_op | source)
XLA Modules:
  0.0 639.0 jit_solution(7620324804941043654)
XLA Ops:
  11.1 2.8 convolution_convert_fusion.4
  13.9 2.9 convolution_convert_fusion.5
  23.7 58.6 %while.26 = (s32[]{:T(128)}, bf16[4,512,192]{1,2,0:T(8,128)(2,1)}, f32[4,3,512]{2,1,0:T(4,128)}, s32[4]{0:T(128)S(1)}, bf16[3072,192]{0,1:T(8,128)(2,1)S(1)}, /*...) while((s32[]{:T(128)}, bf16[4,512,192]{1,2,0:T(8,128)(2,1)}, ...), condition=%wide.region_5.6_spmd, body=%wide.region_2.5_spmd.sunk | while | flops 638585344 | bytes 36271876 | solution.py:251
  30.0 3.1 fusion.207
  33.1 3.9 fusion.208
  44.7 3.1 fusion.207
  47.8 3.9 fusion.208
  59.3 3.1 fusion.207
  62.4 3.9 fusion.208
  74.0 3.1 fusion.207
  77.1 3.9 fusion.208
  84.1 3.7 convolution_convert_fusion.2
  88.1 71.0 %all-reduce.9.cloned.1.call-done = bf16[2048,768]{1,0:T(8,128)(2,1)} async-done(((bf16[2048,768]{1,0:T(8,128)(2,1)}), bf16[2048,768]{1,0:T(8,128)(2,1)}) %all-reduce.9.cloned.1.call-update) | async-done | bytes 3145744 | tf_op jit(solution)/shard_map/psum | solution.py:253
  159.1 3.9 fusion.35
  165.4 2.6 multiply_convert_fusion.1
  168.0 19.9 %convolution_convert_fusion.1 = bf16[2048,768]{1,0:T(8,128)(2,1)} fusion(bf16[768,768]{1,0:T(8,128)(2,1)S(1)} %copy-done.48, bf16[2048,768]{1,0:T(8,128)(2,1)} %multiply_convert_fusion.1, bf16[768,768]{1,0:T(8,128)(2,1)S(1)} %copy-done), kind=kOutput, calls=%fused_computation.101 | convolution fusion | flops 4935647232 | bytes 8650752 | tf_op jit(solution)/shard_map/dot_general | solution.py:261
  188.4 7.1 %fusion.131 = f32[2048,768]{1,0:T(8,128)} fusion(bf16[2048,768]{1,0:T(8,128)(2,1)} %multiply_convert_fusion.1, bf16[768,768]{1,0:T(8,128)(2,1)S(1)} %copy-done), kind=kOutput, calls=%fused_computation.218 | convolution fusion | flops 2415919104 | bytes 10616832 | tf_op jit(solution)/shard_map/dot_general | solution.py:269
  195.5 61.1 %all-reduce.11.cloned.1.call-done = bf16[2048,768]{1,0:T(8,128)(2,1)} async-done(((bf16[2048,768]{1,0:T(8,128)(2,1)}), bf16[2048,768]{1,0:T(8,128)(2,1)}) %all-reduce.11.cloned.1.call-update) | async-done | bytes 3145744 | tf_op jit(solution)/shard_map/psum | solution.py:260
  256.6 5.9 fusion.58
  263.1 2.8 multiply_reduce_fusion.3
  266.0 4.6 fusion.24
  270.7 2.6 copy-done.19
  273.3 4.1 subtract_multiply_fusion.1
  277.4 22.6 %convolution_convert_fusion = bf16[2048,768]{1,0:T(8,128)(2,1)} fusion(bf16[768,768]{1,0:T(8,128)(2,1)S(1)} %copy-done, f32[2048,768]{1,0:T(8,128)} %fusion.131, bf16[768,768]{1,0:T(8,128)(2,1)S(1)} %copy-done.48, f32[2048,768]{1,0:T(8,128)} %subtract_multiply_fusion.1), kind=kOutput, calls=%fused_computation.100 | convolution fusion | flops 4948230144 | bytes 18087936 | tf_op jit(solution)/shard_map/dot_general | solution.py:40
  300.0 68.6 %all-reduce.13.cloned.1.call-done = bf16[2048,768]{1,0:T(8,128)(2,1)} async-done(((bf16[2048,768]{1,0:T(8,128)(2,1)}), bf16[2048,768]{1,0:T(8,128)(2,1)}) %all-reduce.13.cloned.1.call-update) | async-done | bytes 3145744 | tf_op jit(solution)/shard_map/psum | solution.py:274
  368.7 8.4 %fusion.59 = (f32[2048]{0:T(1024)S(1)}, f32[2048]{0:T(1024)S(1)}) fusion(f32[768]{0:T(1024)S(1)} %copy-done.38, f32[2048,768]{1,0:T(8,128)} %subtract_multiply_fusion.1, bf16[2048,768]{1,0:T(8,128)(2,1)} %all-reduce.13.cloned.1.call-done, f32[2048]{0:T(1024)S(1)} %add_rsqrt_fusion.1, f32[2048]{0:T(1024)S(1)} %copy-done.33, ...), kind=kLoop, calls=%fused_computation.123 | loop fusion | flops 17297408 | bytes 15764480 | tf_op jit(solution)/shard_map/reduce_sum | solution.py:26
  377.1 5.2 subtract_multiply_fusion
  382.4 2.8 fusion.48
  388.6 154.5 %while.27 = (s32[]{:T(128)}, f32[3072,192]{0,1:T(8,128)}, f32[3072,192]{0,1:T(8,128)S(1)}, bf16[4,512,192]{1,2,0:T(8,128)(2,1)}, s32[4]{0:T(128)}, /*index=5*/bf...) while((s32[]{:T(128)}, f32[3072,192]{0,1:T(8,128)}, ...), condition=%wide.region_19.20_spmd, body=%wide.region_17.19_spmd.sunk | while | flops 1536195072 | bytes 170713200 | solution.py:311
  400.6 6.7 %multiply_reduce_fusion.6 = (f32[3,512]{1,0:T(4,128)S(1)}, f32[3,512,1536]{2,1,0:T(8,128)}) fusion(f32[3,512,1536]{2,1,0:T(8,128)S(1)} %fusion.220, f32[3,512]{1,0:T(4,128)S(1)} %dynamic-slice_bitcast_fusion.2, bf16[512,3,64]{0,2,1:T(8,128)(2,1)S(1)} %bitcast.166, bf16[1536,3,64]{0,2,1:T(8,128)(2,1)S(1)} %bitcast.162, ...), kind=kOutput, calls=%fused_computation.21.clone.1 | convolution fusion | flops 316144128 | bytes 20459520 | tf_op jit(solution)/shard_map/while/body/eval_jaxpr/qhd,khd->hqk/dot_general | solution.py:72
  407.3 9.4 %multiply_convert_fusion.3 = bf16[3,512,1536]{2,1,0:T(8,128)(2,1)} fusion(f32[3,512,1536]{2,1,0:T(8,128)} %get-tuple-element.368, f32[3,512,1536]{2,1,0:T(8,128)} %copy-done.2, f32[3,512]{1,0:T(4,128)S(1)} %get-tuple-element.369), kind=kLoop, calls=%fused_computation.20.clone.1 | loop fusion | flops 7077888 | bytes 23599104 | tf_op jit(solution)/shard_map/while/body/eval_jaxpr/convert_element_type | solution.py:153
  416.7 4.9 fusion.221
  439.2 6.7 %multiply_reduce_fusion.6 = (f32[3,512]{1,0:T(4,128)S(1)}, f32[3,512,1536]{2,1,0:T(8,128)}) fusion(f32[3,512,1536]{2,1,0:T(8,128)S(1)} %fusion.220, f32[3,512]{1,0:T(4,128)S(1)} %dynamic-slice_bitcast_fusion.2, bf16[512,3,64]{0,2,1:T(8,128)(2,1)S(1)} %bitcast.166, bf16[1536,3,64]{0,2,1:T(8,128)(2,1)S(1)} %bitcast.162, ...), kind=kOutput, calls=%fused_computation.21.clone.1 | convolution fusion | flops 316144128 | bytes 20459520 | tf_op jit(solution)/shard_map/while/body/eval_jaxpr/qhd,khd->hqk/dot_general | solution.py:72
  445.9 9.4 %multiply_convert_fusion.3 = bf16[3,512,1536]{2,1,0:T(8,128)(2,1)} fusion(f32[3,512,1536]{2,1,0:T(8,128)} %get-tuple-element.368, f32[3,512,1536]{2,1,0:T(8,128)} %copy-done.2, f32[3,512]{1,0:T(4,128)S(1)} %get-tuple-element.369), kind=kLoop, calls=%fused_computation.20.clone.1 | loop fusion | flops 7077888 | bytes 23599104 | tf_op jit(solution)/shard_map/while/body/eval_jaxpr/convert_element_type | solution.py:153
  455.3 4.9 fusion.221
  477.8 6.7 %multiply_reduce_fusion.6 = (f32[3,512]{1,0:T(4,128)S(1)}, f32[3,512,1536]{2,1,0:T(8,128)}) fusion(f32[3,512,1536]{2,1,0:T(8,128)S(1)} %fusion.220, f32[3,512]{1,0:T(4,128)S(1)} %dynamic-slice_bitcast_fusion.2, bf16[512,3,64]{0,2,1:T(8,128)(2,1)S(1)} %bitcast.166, bf16[1536,3,64]{0,2,1:T(8,128)(2,1)S(1)} %bitcast.162, ...), kind=kOutput, calls=%fused_computation.21.clone.1 | convolution fusion | flops 316144128 | bytes 20459520 | tf_op jit(solution)/shard_map/while/body/eval_jaxpr/qhd,khd->hqk/dot_general | solution.py:72
  484.5 9.4 %multiply_convert_fusion.3 = bf16[3,512,1536]{2,1,0:T(8,128)(2,1)} fusion(f32[3,512,1536]{2,1,0:T(8,128)} %get-tuple-element.368, f32[3,512,1536]{2,1,0:T(8,128)} %copy-done.2, f32[3,512]{1,0:T(4,128)S(1)} %get-tuple-element.369), kind=kLoop, calls=%fused_computation.20.clone.1 | loop fusion | flops 7077888 | bytes 23599104 | tf_op jit(solution)/shard_map/while/body/eval_jaxpr/convert_element_type | solution.py:153
  493.9 4.9 fusion.221
  516.3 6.7 %multiply_reduce_fusion.6 = (f32[3,512]{1,0:T(4,128)S(1)}, f32[3,512,1536]{2,1,0:T(8,128)}) fusion(f32[3,512,1536]{2,1,0:T(8,128)S(1)} %fusion.220, f32[3,512]{1,0:T(4,128)S(1)} %dynamic-slice_bitcast_fusion.2, bf16[512,3,64]{0,2,1:T(8,128)(2,1)S(1)} %bitcast.166, bf16[1536,3,64]{0,2,1:T(8,128)(2,1)S(1)} %bitcast.162, ...), kind=kOutput, calls=%fused_computation.21.clone.1 | convolution fusion | flops 316144128 | bytes 20459520 | tf_op jit(solution)/shard_map/while/body/eval_jaxpr/qhd,khd->hqk/dot_general | solution.py:72
  523.1 9.4 %multiply_convert_fusion.3 = bf16[3,512,1536]{2,1,0:T(8,128)(2,1)} fusion(f32[3,512,1536]{2,1,0:T(8,128)} %get-tuple-element.368, f32[3,512,1536]{2,1,0:T(8,128)} %copy-done.2, f32[3,512]{1,0:T(4,128)S(1)} %get-tuple-element.369), kind=kLoop, calls=%fused_computation.20.clone.1 | loop fusion | flops 7077888 | bytes 23599104 | tf_op jit(solution)/shard_map/while/body/eval_jaxpr/convert_element_type | solution.py:153
  532.4 4.9 fusion.221
  546.8 4.6 fusion.133
  552.6 7.9 %add_convert_fusion = bf16[2048,768]{1,0:T(8,128)(2,1)} fusion(f32[2048,768]{1,0:T(8,128)} %fusion.133, f32[2048,768]{1,0:T(8,128)S(1)} %fusion.125, f32[2048,768]{1,0:T(8,128)S(1)} %fusion.132, f32[2048,768]{1,0:T(8,128)S(1)} %fusion.62, f32[2048,8]{0,1:T(8,128)S(1)} %convolution_multiply_fusion.4, bf16[768,8]{0,1:T(8,128)(2,1)S(1)} %copy-done.40), kind=kOutput, calls=%fused_computation.50 | convolution fusion | flops 158859264 | bytes 28389376 | tf_op jit(solution)/shard_map/dot_general | solution.py:332
  562.5 2.5 fusion.61
  565.0 2.2 convolution_multiply_fusion.7
  570.4 37.0 %all-reduce.3 = (f32[8,3,64]{2,1,0:T(4,128)S(1)}, f32[8,3,64]{2,1,0:T(4,128)S(1)}) all-reduce(f32[8,3,64]{2,1,0:T(4,128)S(1)} %reshape.273, f32[8,3,64]{2,1,0:T(4,128)S(1)} %reshape.274), channel_id=2, replica_groups=mesh['dp'=8,'tensor'=4] {'dp'}, use_global_device_ids=true, to_apply=%region_21.22.clone | all-reduce | flops 3072 | bytes 24576
  608.7 20.5 %all-reduce.15.cloned.1.call-done = bf16[2048,768]{1,0:T(8,128)(2,1)} async-done(((bf16[2048,768]{1,0:T(8,128)(2,1)}), bf16[2048,768]{1,0:T(8,128)(2,1)}) %all-reduce.15.cloned.1.call-update) | async-done | bytes 3145744 | tf_op jit(solution)/shard_map/psum | solution.py:338
  629.2 2.9 dynamic-slice_add_fusion
  (314 shorter events, 119.5 us)
Async XLA Ops:
  7.2 160.8 %copy-start = (bf16[768,768]{1,0:T(8,128)(2,1)S(1)}, bf16[768,768]{1,0:T(8,128)(2,1)}, u32[]{:S(2)}) copy-start(bf16[768,768]{1,0:T(8,128)(2,1)} %param.25) | copy-start | bytes 3538948
  7.2 9.6 %copy-start.36 = (bf16[768,192]{0,1:T(8,128)(2,1)S(1)}, bf16[768,192]{0,1:T(8,128)(2,1)}, u32[]{:S(2)}) copy-start(bf16[768,192]{0,1:T(8,128)(2,1)} %param.22) | copy-start | bytes 884740
  7.2 151.9 %all-reduce.9.cloned.1.call-start = ((), (), s32[]{:S(2)}) async-start(), calls=%async_computation | async-start | bytes 6291456 | tf_op jit(solution)/shard_map/psum | solution.py:253
  9.0 11.1 %copy-start.44 = (bf16[8,192]{1,0:T(8,128)(2,1)}, bf16[8,192]{1,0:T(8,128)(2,1)S(1)}, u32[]{:S(2)}) copy-start(bf16[8,192]{1,0:T(8,128)(2,1)S(1)} %reshape.272) | copy-start | bytes 9220
  9.8 8.2 %copy-start.46 = (bf16[8,192]{1,0:T(8,128)(2,1)}, bf16[8,192]{1,0:T(8,128)(2,1)S(1)}, u32[]{:S(2)}) copy-start(bf16[8,192]{1,0:T(8,128)(2,1)S(1)} %reshape.269) | copy-start | bytes 9220
  9.8 7.0 %copy-start.4 = (bf16[2048,768]{1,0:T(8,128)(2,1)S(1)}, bf16[2048,768]{1,0:T(8,128)(2,1)}, u32[]{:S(2)}) copy-start(bf16[2048,768]{1,0:T(8,128)(2,1)} %param.19) | copy-start | bytes 9437188
  13.9 6.2 copy-start.35
  13.9 4.5 copy-start.28
  82.3 80.7 %copy-start.17 = (bf16[3072,192]{0,1:T(8,128)(2,1)}, bf16[3072,192]{0,1:T(8,128)(2,1)S(1)}, u32[]{:S(2)}) copy-start(bf16[3072,192]{0,1:T(8,128)(2,1)S(1)} %get-tuple-element.479) | copy-start | bytes 3538948
  82.3 80.7 %copy-start.18 = (bf16[3072,192]{0,1:T(8,128)(2,1)}, bf16[3072,192]{0,1:T(8,128)(2,1)S(1)}, u32[]{:S(2)}) copy-start(bf16[3072,192]{0,1:T(8,128)(2,1)S(1)} %get-tuple-element.480) | copy-start | bytes 3538948
  87.8 77.6 %copy-start.38 = (f32[768]{0:T(1024)S(1)}, f32[768]{0:T(1024)}, u32[]{:S(2)}) copy-start(f32[768]{0:T(1024)} %param.27) | copy-start | bytes 9220
  87.8 168.8 %all-reduce.11.cloned.1.call-start = ((), (), s32[]{:S(2)}) async-start(), calls=%async_computation.1 | async-start | bytes 6291456 | tf_op jit(solution)/shard_map/psum | solution.py:260
  159.1 4.7 copy-start.8
  187.9 68.7 %copy-start.33 = (f32[2048]{0:T(1024)S(1)}, f32[2048]{0:T(1024)}, u32[]{:S(2)}) copy-start(f32[2048]{0:T(1024)} %copy-done.32) | copy-start | bytes 24580
  187.9 180.8 %all-reduce.13.cloned.1.call-start = ((), (), s32[]{:S(2)}) async-start(), calls=%async_computation.2 | async-start | bytes 6291456 | tf_op jit(solution)/shard_map/psum | solution.py:274
  256.6 5.9 copy-start.6
  256.6 5.9 copy-start.9
  256.6 6.5 %copy-start.21 = (bf16[2048,768]{1,0:T(8,128)(2,1)S(1)}, bf16[2048,768]{1,0:T(8,128)(2,1)}, u32[]{:S(2)}) copy-start(bf16[2048,768]{1,0:T(8,128)(2,1)} %all-reduce.11.cloned.1.call-done) | copy-start | bytes 9437188
  300.0 329.2 %all-reduce.15.cloned.1.call-start = ((), (), s32[]{:S(2)}) async-start(), calls=%async_computation.3 | async-start | bytes 6291456 | tf_op jit(solution)/shard_map/psum | solution.py:338
  368.7 8.4 %copy-start.7 = (bf16[2048,768]{1,0:T(8,128)(2,1)S(1)}, bf16[2048,768]{1,0:T(8,128)(2,1)}, u32[]{:S(2)}) copy-start(bf16[2048,768]{1,0:T(8,128)(2,1)} %param.19) | copy-start | bytes 9437188
  368.7 8.4 %copy-start.10 = (bf16[2048,768]{1,0:T(8,128)(2,1)S(1)}, bf16[2048,768]{1,0:T(8,128)(2,1)}, u32[]{:S(2)}) copy-start(bf16[2048,768]{1,0:T(8,128)(2,1)} %all-reduce.9.cloned.1.call-done) | copy-start | bytes 9437188
  368.7 8.4 %copy-start.26 = (bf16[2048,768]{1,0:T(8,128)(2,1)S(1)}, bf16[2048,768]{1,0:T(8,128)(2,1)}, u32[]{:S(2)}) copy-start(bf16[2048,768]{1,0:T(8,128)(2,1)} %all-reduce.13.cloned.1.call-done) | copy-start | bytes 9437188
  377.1 5.3 copy-start.31
  382.4 6.2 copy-start.20
  388.6 154.5 %copy-start.47 = (bf16[8,192]{1,0:T(8,128)(2,1)S(1)}, bf16[8,192]{1,0:T(8,128)(2,1)}, u32[]{:S(2)}) copy-start(bf16[8,192]{1,0:T(8,128)(2,1)} %copy-done.46) | copy-start | bytes 9220
  400.6 6.7 %copy-start.2 = (f32[3,512,1536]{2,1,0:T(8,128)}, f32[3,512,1536]{2,1,0:T(8,128)S(1)}, u32[]{:S(2)}) copy-start(f32[3,512,1536]{2,1,0:T(8,128)S(1)} %fusion.220) | copy-start | bytes 28311556 | tf_op jit(solution)/shard_map/while
  416.7 5.1 copy-start.3
  416.7 5.3 copy-start.12
  416.7 6.8 %copy-start.23 = (bf16[512,192]{0,1:T(8,128)(2,1)S(1)}, bf16[512,192]{0,1:T(8,128)(2,1)}, u32[]{:S(2)}) copy-start(bf16[512,192]{0,1:T(8,128)(2,1)} %copy-done.22) | copy-start | bytes 589828 | tf_op jit(solution)/shard_map/while
  439.2 6.7 %copy-start.2 = (f32[3,512,1536]{2,1,0:T(8,128)}, f32[3,512,1536]{2,1,0:T(8,128)S(1)}, u32[]{:S(2)}) copy-start(f32[3,512,1536]{2,1,0:T(8,128)S(1)} %fusion.220) | copy-start | bytes 28311556 | tf_op jit(solution)/shard_map/while
  455.3 5.1 copy-start.3
  455.3 5.3 copy-start.12
  455.3 6.8 %copy-start.23 = (bf16[512,192]{0,1:T(8,128)(2,1)S(1)}, bf16[512,192]{0,1:T(8,128)(2,1)}, u32[]{:S(2)}) copy-start(bf16[512,192]{0,1:T(8,128)(2,1)} %copy-done.22) | copy-start | bytes 589828 | tf_op jit(solution)/shard_map/while
  473.4 4.4 copy-start.22
  477.7 6.7 %copy-start.2 = (f32[3,512,1536]{2,1,0:T(8,128)}, f32[3,512,1536]{2,1,0:T(8,128)S(1)}, u32[]{:S(2)}) copy-start(f32[3,512,1536]{2,1,0:T(8,128)S(1)} %fusion.220) | copy-start | bytes 28311556 | tf_op jit(solution)/shard_map/while
  493.9 5.1 copy-start.3
  493.9 5.3 copy-start.12
  493.9 6.8 %copy-start.23 = (bf16[512,192]{0,1:T(8,128)(2,1)S(1)}, bf16[512,192]{0,1:T(8,128)(2,1)}, u32[]{:S(2)}) copy-start(bf16[512,192]{0,1:T(8,128)(2,1)} %copy-done.22) | copy-start | bytes 589828 | tf_op jit(solution)/shard_map/while
  516.3 6.7 %copy-start.2 = (f32[3,512,1536]{2,1,0:T(8,128)}, f32[3,512,1536]{2,1,0:T(8,128)S(1)}, u32[]{:S(2)}) copy-start(f32[3,512,1536]{2,1,0:T(8,128)S(1)} %fusion.220) | copy-start | bytes 28311556 | tf_op jit(solution)/shard_map/while
  532.4 5.1 copy-start.3
  532.4 5.3 copy-start.12
  532.4 6.8 %copy-start.23 = (bf16[512,192]{0,1:T(8,128)(2,1)S(1)}, bf16[512,192]{0,1:T(8,128)(2,1)}, u32[]{:S(2)}) copy-start(bf16[512,192]{0,1:T(8,128)(2,1)} %copy-done.22) | copy-start | bytes 589828 | tf_op jit(solution)/shard_map/while
  545.5 5.9 copy-start.24
  545.8 5.7 copy-start.16
  545.8 5.7 copy-start.37
  552.5 8.7 %copy-start.49 = (u32[32]{0:T(128)S(1)}, u32[32]{0:T(128)}, u32[]{:S(2)}) copy-start(u32[32]{0:T(128)} %constant.161) | copy-start | bytes 388
  552.5 10.0 %copy-start.43 = (f32[768]{0:T(1024)S(1)}, f32[768]{0:T(1024)}, u32[]{:S(2)}) copy-start(f32[768]{0:T(1024)} %param.28) | copy-start | bytes 9220
  552.6 79.5 %copy-start.1 = (bf16[768,768]{1,0:T(8,128)(2,1)S(1)}, bf16[768,768]{1,0:T(8,128)(2,1)}, u32[]{:S(2)}) copy-start(bf16[768,768]{1,0:T(8,128)(2,1)} %param.25) | copy-start | bytes 3538948
  (33 other events, 88.0 us)
Sparse Core Ops, SparseCore 0:
  87.9 71.1 all-reduce.8
  188.0 68.5 all-reduce.10
  300.1 68.5 all-reduce.12
  560.6 68.5 all-reduce.14
where the time goes:
time: 649 us; the launch traced here: 639 us
  waiting for transfers between devices  221 us (34%)
  matrix products  173 us (27%)
  other arithmetic  109 us (17%)
  local copies, waits for them, and re-layouts  70.4 us (11%)
  blocking collectives  37 us (6%)
  between operations  15.5 us (2%)
  loops' own time  12.2 us (2%)
    psum x1, waiting for transfers between devices, on_device(): lax.psum(jnp.dot(context, w_out, preferred_element_type=jnp.float32).asty...  71 us
    psum x1, waiting for transfers between devices, on_device(): lax.psum(transpose_dot(grad_pre, w_inner).astype(jnp.bfloat16), 'tensor')  68.6 us
    psum x1, waiting for transfers between devices, on_device(): lax.psum(jnp.dot(active, w_ffn_out, preferred_element_type=jnp.float32).a...  61.1 us
    convert_element_type x4, other arithmetic, attend_backward(): grad_scores = (probability * (grad_prob - row_delta)).astype(jnp.bfloat16)  37.5 us
    unnamed x1, blocking collectives  37 us
    dot_general x8, matrix products, block_scores(): jnp.einsum('qhd,khd->hqk', query_block, key_block, preferred_element_type...  34.9 us
    dot_general x7, matrix products, transpose_dot(): lax.dot_general(left_side, right_side, (((1,), (1,)), ((), ())), preferre...  30 us
    psum x1, waiting for transfers between devices, on_device(): lax.psum(input_term.astype(jnp.bfloat16), 'tensor').astype(jnp.float32)  20.5 us
  transfers between devices with their start and end apart: 4, of which 4 were waited for; matrix products, arithmetic and copies ran while one was open for 3% of the time, Pallas kernels for 0%

commit v1 on v0

--- a/solution.py
+++ b/solution.py
@@ -9,6 +9,7 @@
 SEQ = 512
 EPSILON = 1e-05
 NEGATIVE = -1e30
+detail_classes = lambda mine_x, axis_tag: jax.lax.all_gather(mine_x, axis_name=axis_tag).sum(axis=0)
 
 
 def normalize(vector, scale_gain):
@@ -250,7 +251,7 @@
 
     context_blocks, log_total = lax.map(forward_block, jnp.arange(block_count))
     context = context_blocks.reshape(row_count, col_width).astype(jnp.bfloat16)
-    attn_out = lax.psum(
+    attn_out = detail_classes(
         jnp.dot(context, w_out, preferred_element_type=jnp.float32).astype(jnp.bfloat16), "tensor"
     ).astype(jnp.float32)
     normed, unit_one, inverse_one = normalize(tokens.astype(jnp.float32) + attn_out, gain_attn)

time: 649 us -> 673 us (1.037)
  waiting for transfers between devices: 221 us -> 235 us
  other arithmetic: 109 us -> 118 us
    all_gather x0 -> x1, waiting for transfers between devices: none -> 84.7 us  [jax.lax.all_gather(mine_x, axis_name=axis_tag).sum(axis=0)]
    psum x1 -> x0, waiting for transfers between devices: 71 us -> none  [on_device(): lax.psum(jnp.dot(context, w_out, preferred_element_type=jnp.float32).asty...]
    reduce_sum x0 -> x1, other arithmetic: none -> 8.95 us  [jax.lax.all_gather(mine_x, axis_name=axis_tag).sum(axis=0)]
where the time goes in v1:
time: 673 us; the launch traced here: 663 us
  waiting for transfers between devices  235 us (35%)
  matrix products  173 us (26%)
  other arithmetic  118 us (18%)
  local copies, waits for them, and re-layouts  70.8 us (11%)
  blocking collectives  37 us (5%)
  between operations  15.5 us (2%)
  loops' own time  13.4 us (2%)
    all_gather x1, waiting for transfers between devices, jax.lax.all_gather(mine_x, axis_name=axis_tag).sum(axis=0)  84.7 us
    psum x1, waiting for transfers between devices, on_device(): lax.psum(transpose_dot(grad_pre, w_inner).astype(jnp.bfloat16), 'tensor')  68.7 us
    psum x1, waiting for transfers between devices, on_device(): lax.psum(jnp.dot(active, w_ffn_out, preferred_element_type=jnp.float32).a...  61 us
    convert_element_type x4, other arithmetic, attend_backward(): grad_scores = (probability * (grad_prob - row_delta)).astype(jnp.bfloat16)  37.6 us
    unnamed x1, blocking collectives  37 us
    dot_general x8, matrix products, block_scores(): jnp.einsum('qhd,khd->hqk', query_block, key_block, preferred_element_type...  34.9 us
    dot_general x7, matrix products, transpose_dot(): lax.dot_general(left_side, right_side, (((1,), (1,)), ((), ())), preferre...  30 us
    psum x1, waiting for transfers between devices, on_device(): lax.psum(input_term.astype(jnp.bfloat16), 'tensor').astype(jnp.float32)  20.5 us
  transfers between devices with their start and end apart: 4, of which 4 were waited for; matrix products, arithmetic and copies ran while one was open for 3% of the time, Pallas kernels for 0%

profile of v1, /device:TPU:0, one launch (start us, length us, event | category | flops | bytes accessed | tf_op | source)
XLA Modules:
  0.0 663.4 jit_solution(4611505856906981641)
XLA Ops:
  11.1 2.8 convolution_convert_fusion.4
  13.9 2.9 convolution_convert_fusion.5
  23.7 59.4 %while.26 = (s32[]{:T(128)}, bf16[4,512,192]{1,2,0:T(8,128)(2,1)}, f32[4,3,512]{2,1,0:T(4,128)}, s32[4]{0:T(128)S(1)}, bf16[3072,192]{0,1:T(8,128)(2,1)S(1)}, /*...) while((s32[]{:T(128)}, bf16[4,512,192]{1,2,0:T(8,128)(2,1)}, ...), condition=%wide.region_5.6_spmd, body=%wide.region_2.5_spmd.sunk | while | flops 638585344 | bytes 36271876 | solution.py:252
  30.2 3.1 fusion.207
  33.3 3.9 fusion.208
  45.1 3.1 fusion.207
  48.2 3.9 fusion.208
  59.9 3.1 fusion.207
  63.0 3.9 fusion.208
  74.8 3.1 fusion.207
  77.9 3.9 fusion.208
  84.9 3.7 convolution_convert_fusion.2
  88.8 84.7 %all-gather.3.cloned.1.call-done = bf16[8192,768]{1,0:T(8,128)(2,1)} async-done(((bf16[2048,768]{1,0:T(8,128)(2,1)}), bf16[8192,768]{1,0:T(8,128)(2,1)}) %all-gather.3.cloned.1.call-update) | async-done | bytes 12582928 | tf_op jit(solution)/shard_map/all_gather | solution.py:12
  173.5 8.9 %reduce_sum.114 = bf16[2048,768]{1,0:T(8,128)(2,1)} reduce(bf16[4,2048,768]{2,1,0:T(8,128)(2,1)} %bitcast.175, bf16[]{:T(256)} %constant.86.clone.1), dimensions={0}, to_apply=%region_6.7 | reduce | flops 4718592 | bytes 15728642 | tf_op jit(solution)/shard_map/reduce_sum | solution.py:12
  182.5 3.9 fusion.35
  188.8 2.6 multiply_convert_fusion.1
  191.4 19.9 %convolution_convert_fusion.1 = bf16[2048,768]{1,0:T(8,128)(2,1)} fusion(bf16[768,768]{1,0:T(8,128)(2,1)S(1)} %copy-done.46, bf16[2048,768]{1,0:T(8,128)(2,1)} %multiply_convert_fusion.1, bf16[768,768]{1,0:T(8,128)(2,1)S(1)} %copy-done), kind=kOutput, calls=%fused_computation.101 | convolution fusion | flops 4935647232 | bytes 8650752 | tf_op jit(solution)/shard_map/dot_general | solution.py:262
  211.8 7.1 %fusion.131 = f32[2048,768]{1,0:T(8,128)} fusion(bf16[2048,768]{1,0:T(8,128)(2,1)} %multiply_convert_fusion.1, bf16[768,768]{1,0:T(8,128)(2,1)S(1)} %copy-done), kind=kOutput, calls=%fused_computation.218 | convolution fusion | flops 2415919104 | bytes 10616832 | tf_op jit(solution)/shard_map/dot_general | solution.py:270
  218.9 61.0 %all-reduce.8.cloned.1.call-done = bf16[2048,768]{1,0:T(8,128)(2,1)} async-done(((bf16[2048,768]{1,0:T(8,128)(2,1)}), bf16[2048,768]{1,0:T(8,128)(2,1)}) %all-reduce.8.cloned.1.call-update) | async-done | bytes 3145744 | tf_op jit(solution)/shard_map/psum | solution.py:261
  279.9 5.9 fusion.58
  286.4 2.8 multiply_reduce_fusion.3
  289.3 4.6 fusion.24
  294.0 2.6 copy-done.19
  296.5 4.1 subtract_multiply_fusion.1
  300.7 22.6 %convolution_convert_fusion = bf16[2048,768]{1,0:T(8,128)(2,1)} fusion(bf16[768,768]{1,0:T(8,128)(2,1)S(1)} %copy-done, f32[2048,768]{1,0:T(8,128)} %fusion.131, bf16[768,768]{1,0:T(8,128)(2,1)S(1)} %copy-done.46, f32[2048,768]{1,0:T(8,128)} %subtract_multiply_fusion.1), kind=kOutput, calls=%fused_computation.100 | convolution fusion | flops 4948230144 | bytes 18087936 | tf_op jit(solution)/shard_map/dot_general | solution.py:41
  323.4 68.7 %all-reduce.10.cloned.1.call-done = bf16[2048,768]{1,0:T(8,128)(2,1)} async-done(((bf16[2048,768]{1,0:T(8,128)(2,1)}), bf16[2048,768]{1,0:T(8,128)(2,1)}) %all-reduce.10.cloned.1.call-update) | async-done | bytes 3145744 | tf_op jit(solution)/shard_map/psum | solution.py:275
  392.0 8.3 %fusion.59 = (f32[2048]{0:T(1024)S(1)}, f32[2048]{0:T(1024)S(1)}) fusion(f32[768]{0:T(1024)S(1)} %copy-done.36, f32[2048,768]{1,0:T(8,128)} %subtract_multiply_fusion.1, bf16[2048,768]{1,0:T(8,128)(2,1)} %all-reduce.10.cloned.1.call-done, f32[2048]{0:T(1024)S(1)} %add_rsqrt_fusion.1, f32[2048]{0:T(1024)S(1)} %broadcast_multiply_fusion.5, ...), kind=kLoop, calls=%fused_computation.123 | loop fusion | flops 17297408 | bytes 15764480 | tf_op jit(solution)/shard_map/reduce_sum | solution.py:27
  400.4 5.2 subtract_multiply_fusion
  405.7 2.8 fusion.48
  411.8 155.6 %while.27 = (s32[]{:T(128)}, f32[3072,192]{0,1:T(8,128)}, f32[3072,192]{0,1:T(8,128)S(1)}, bf16[4,512,192]{1,2,0:T(8,128)(2,1)}, s32[4]{0:T(128)}, /*index=5*/bf...) while((s32[]{:T(128)}, f32[3072,192]{0,1:T(8,128)}, ...), condition=%wide.region_19.20_spmd, body=%wide.region_17.19_spmd.sunk | while | flops 1536195072 | bytes 170713200 | solution.py:312
  424.1 6.7 %multiply_reduce_fusion.6 = (f32[3,512]{1,0:T(4,128)S(1)}, f32[3,512,1536]{2,1,0:T(8,128)}) fusion(f32[3,512,1536]{2,1,0:T(8,128)S(1)} %fusion.220, f32[3,512]{1,0:T(4,128)S(1)} %dynamic-slice_bitcast_fusion.2, bf16[512,3,64]{0,2,1:T(8,128)(2,1)S(1)} %bitcast.167, bf16[1536,3,64]{0,2,1:T(8,128)(2,1)S(1)} %bitcast.163, ...), kind=kOutput, calls=%fused_computation.21.clone.1 | convolution fusion | flops 316144128 | bytes 20459520 | tf_op jit(solution)/shard_map/while/body/eval_jaxpr/qhd,khd->hqk/dot_general | solution.py:73
  430.9 9.4 %multiply_convert_fusion.3 = bf16[3,512,1536]{2,1,0:T(8,128)(2,1)} fusion(f32[3,512,1536]{2,1,0:T(8,128)} %get-tuple-element.368, f32[3,512,1536]{2,1,0:T(8,128)} %copy-done.2, f32[3,512]{1,0:T(4,128)S(1)} %get-tuple-element.369), kind=kLoop, calls=%fused_computation.20.clone.1 | loop fusion | flops 7077888 | bytes 23599104 | tf_op jit(solution)/shard_map/while/body/eval_jaxpr/convert_element_type | solution.py:154
  440.3 4.9 fusion.221
  463.0 6.7 %multiply_reduce_fusion.6 = (f32[3,512]{1,0:T(4,128)S(1)}, f32[3,512,1536]{2,1,0:T(8,128)}) fusion(f32[3,512,1536]{2,1,0:T(8,128)S(1)} %fusion.220, f32[3,512]{1,0:T(4,128)S(1)} %dynamic-slice_bitcast_fusion.2, bf16[512,3,64]{0,2,1:T(8,128)(2,1)S(1)} %bitcast.167, bf16[1536,3,64]{0,2,1:T(8,128)(2,1)S(1)} %bitcast.163, ...), kind=kOutput, calls=%fused_computation.21.clone.1 | convolution fusion | flops 316144128 | bytes 20459520 | tf_op jit(solution)/shard_map/while/body/eval_jaxpr/qhd,khd->hqk/dot_general | solution.py:73
  469.7 9.4 %multiply_convert_fusion.3 = bf16[3,512,1536]{2,1,0:T(8,128)(2,1)} fusion(f32[3,512,1536]{2,1,0:T(8,128)} %get-tuple-element.368, f32[3,512,1536]{2,1,0:T(8,128)} %copy-done.2, f32[3,512]{1,0:T(4,128)S(1)} %get-tuple-element.369), kind=kLoop, calls=%fused_computation.20.clone.1 | loop fusion | flops 7077888 | bytes 23599104 | tf_op jit(solution)/shard_map/while/body/eval_jaxpr/convert_element_type | solution.py:154
  479.1 4.9 fusion.221
  501.8 6.7 %multiply_reduce_fusion.6 = (f32[3,512]{1,0:T(4,128)S(1)}, f32[3,512,1536]{2,1,0:T(8,128)}) fusion(f32[3,512,1536]{2,1,0:T(8,128)S(1)} %fusion.220, f32[3,512]{1,0:T(4,128)S(1)} %dynamic-slice_bitcast_fusion.2, bf16[512,3,64]{0,2,1:T(8,128)(2,1)S(1)} %bitcast.167, bf16[1536,3,64]{0,2,1:T(8,128)(2,1)S(1)} %bitcast.163, ...), kind=kOutput, calls=%fused_computation.21.clone.1 | convolution fusion | flops 316144128 | bytes 20459520 | tf_op jit(solution)/shard_map/while/body/eval_jaxpr/qhd,khd->hqk/dot_general | solution.py:73
  508.6 9.4 %multiply_convert_fusion.3 = bf16[3,512,1536]{2,1,0:T(8,128)(2,1)} fusion(f32[3,512,1536]{2,1,0:T(8,128)} %get-tuple-element.368, f32[3,512,1536]{2,1,0:T(8,128)} %copy-done.2, f32[3,512]{1,0:T(4,128)S(1)} %get-tuple-element.369), kind=kLoop, calls=%fused_computation.20.clone.1 | loop fusion | flops 7077888 | bytes 23599104 | tf_op jit(solution)/shard_map/while/body/eval_jaxpr/convert_element_type | solution.py:154
  518.0 4.9 fusion.221
  540.7 6.7 %multiply_reduce_fusion.6 = (f32[3,512]{1,0:T(4,128)S(1)}, f32[3,512,1536]{2,1,0:T(8,128)}) fusion(f32[3,512,1536]{2,1,0:T(8,128)S(1)} %fusion.220, f32[3,512]{1,0:T(4,128)S(1)} %dynamic-slice_bitcast_fusion.2, bf16[512,3,64]{0,2,1:T(8,128)(2,1)S(1)} %bitcast.167, bf16[1536,3,64]{0,2,1:T(8,128)(2,1)S(1)} %bitcast.163, ...), kind=kOutput, calls=%fused_computation.21.clone.1 | convolution fusion | flops 316144128 | bytes 20459520 | tf_op jit(solution)/shard_map/while/body/eval_jaxpr/qhd,khd->hqk/dot_general | solution.py:73
  547.4 9.4 %multiply_convert_fusion.3 = bf16[3,512,1536]{2,1,0:T(8,128)(2,1)} fusion(f32[3,512,1536]{2,1,0:T(8,128)} %get-tuple-element.368, f32[3,512,1536]{2,1,0:T(8,128)} %copy-done.2, f32[3,512]{1,0:T(4,128)S(1)} %get-tuple-element.369), kind=kLoop, calls=%fused_computation.20.clone.1 | loop fusion | flops 7077888 | bytes 23599104 | tf_op jit(solution)/shard_map/while/body/eval_jaxpr/convert_element_type | solution.py:154
  556.8 4.9 fusion.221
  571.2 4.6 fusion.133
  576.9 7.9 %add_convert_fusion = bf16[2048,768]{1,0:T(8,128)(2,1)} fusion(f32[2048,768]{1,0:T(8,128)} %fusion.133, f32[2048,768]{1,0:T(8,128)S(1)} %fusion.125, f32[2048,768]{1,0:T(8,128)S(1)} %fusion.132, f32[2048,768]{1,0:T(8,128)S(1)} %fusion.62, f32[2048,8]{0,1:T(8,128)S(1)} %convolution_multiply_fusion.4, bf16[768,8]{0,1:T(8,128)(2,1)S(1)} %copy-done.38), kind=kOutput, calls=%fused_computation.50 | convolution fusion | flops 158859264 | bytes 28389376 | tf_op jit(solution)/shard_map/dot_general | solution.py:333
  586.9 2.5 fusion.61
  594.7 37.0 %all-reduce.3 = (f32[8,3,64]{2,1,0:T(4,128)S(1)}, f32[8,3,64]{2,1,0:T(4,128)S(1)}) all-reduce(f32[8,3,64]{2,1,0:T(4,128)S(1)} %reshape.273, f32[8,3,64]{2,1,0:T(4,128)S(1)} %reshape.274), channel_id=3, replica_groups=mesh['dp'=8,'tensor'=4] {'dp'}, use_global_device_ids=true, to_apply=%region_21.22.clone | all-reduce | flops 3072 | bytes 24576
  633.1 20.5 %all-reduce.12.cloned.1.call-done = bf16[2048,768]{1,0:T(8,128)(2,1)} async-done(((bf16[2048,768]{1,0:T(8,128)(2,1)}), bf16[2048,768]{1,0:T(8,128)(2,1)}) %all-reduce.12.cloned.1.call-update) | async-done | bytes 3145744 | tf_op jit(solution)/shard_map/psum | solution.py:339
  653.6 2.9 dynamic-slice_add_fusion
  (311 shorter events, 122.3 us)
Async XLA Ops:
  7.2 184.2 %copy-start = (bf16[768,768]{1,0:T(8,128)(2,1)S(1)}, bf16[768,768]{1,0:T(8,128)(2,1)}, u32[]{:S(2)}) copy-start(bf16[768,768]{1,0:T(8,128)(2,1)} %param.25) | copy-start | bytes 3538948
  7.2 9.6 %copy-start.34 = (bf16[768,192]{0,1:T(8,128)(2,1)S(1)}, bf16[768,192]{0,1:T(8,128)(2,1)}, u32[]{:S(2)}) copy-start(bf16[768,192]{0,1:T(8,128)(2,1)} %param.22) | copy-start | bytes 884740
  7.2 166.3 %all-gather.3.cloned.1.call-start = ((), (), s32[]{:S(2)}) async-start(), calls=%async_computation.3 | async-start | bytes 15728640 | tf_op jit(solution)/shard_map/all_gather | solution.py:12
  9.0 11.1 %copy-start.42 = (bf16[8,192]{1,0:T(8,128)(2,1)}, bf16[8,192]{1,0:T(8,128)(2,1)S(1)}, u32[]{:S(2)}) copy-start(bf16[8,192]{1,0:T(8,128)(2,1)S(1)} %reshape.272) | copy-start | bytes 9220
  9.8 8.2 %copy-start.44 = (bf16[8,192]{1,0:T(8,128)(2,1)}, bf16[8,192]{1,0:T(8,128)(2,1)S(1)}, u32[]{:S(2)}) copy-start(bf16[8,192]{1,0:T(8,128)(2,1)S(1)} %reshape.269) | copy-start | bytes 9220
  9.8 7.0 %copy-start.4 = (bf16[2048,768]{1,0:T(8,128)(2,1)S(1)}, bf16[2048,768]{1,0:T(8,128)(2,1)}, u32[]{:S(2)}) copy-start(bf16[2048,768]{1,0:T(8,128)(2,1)} %param.19) | copy-start | bytes 9437188
  13.9 6.2 copy-start.33
  13.9 4.5 copy-start.28
  83.1 99.4 %copy-start.17 = (bf16[3072,192]{0,1:T(8,128)(2,1)}, bf16[3072,192]{0,1:T(8,128)(2,1)S(1)}, u32[]{:S(2)}) copy-start(bf16[3072,192]{0,1:T(8,128)(2,1)S(1)} %get-tuple-element.478) | copy-start | bytes 3538948
  83.1 99.4 %copy-start.18 = (bf16[3072,192]{0,1:T(8,128)(2,1)}, bf16[3072,192]{0,1:T(8,128)(2,1)S(1)}, u32[]{:S(2)}) copy-start(bf16[3072,192]{0,1:T(8,128)(2,1)S(1)} %get-tuple-element.479) | copy-start | bytes 3538948
  88.6 191.3 %all-reduce.8.cloned.1.call-start = ((), (), s32[]{:S(2)}) async-start(), calls=%async_computation | async-start | bytes 6291456 | tf_op jit(solution)/shard_map/psum | solution.py:261
  182.5 4.7 copy-start.8
  182.5 6.3 copy-start.36
  211.3 180.7 %all-reduce.10.cloned.1.call-start = ((), (), s32[]{:S(2)}) async-start(), calls=%async_computation.1 | async-start | bytes 6291456 | tf_op jit(solution)/shard_map/psum | solution.py:275
  279.9 5.9 copy-start.6
  279.9 5.9 copy-start.9
  279.9 6.5 copy-start.21
  323.3 330.3 %all-reduce.12.cloned.1.call-start = ((), (), s32[]{:S(2)}) async-start(), calls=%async_computation.2 | async-start | bytes 6291456 | tf_op jit(solution)/shard_map/psum | solution.py:339
  392.0 8.4 %copy-start.7 = (bf16[2048,768]{1,0:T(8,128)(2,1)S(1)}, bf16[2048,768]{1,0:T(8,128)(2,1)}, u32[]{:S(2)}) copy-start(bf16[2048,768]{1,0:T(8,128)(2,1)} %param.19) | copy-start | bytes 9437188
  392.0 8.4 %copy-start.10 = (bf16[2048,768]{1,0:T(8,128)(2,1)S(1)}, bf16[2048,768]{1,0:T(8,128)(2,1)}, u32[]{:S(2)}) copy-start(bf16[2048,768]{1,0:T(8,128)(2,1)} %reduce_sum.114) | copy-start | bytes 9437188
  392.0 8.4 %copy-start.26 = (bf16[2048,768]{1,0:T(8,128)(2,1)S(1)}, bf16[2048,768]{1,0:T(8,128)(2,1)}, u32[]{:S(2)}) copy-start(bf16[2048,768]{1,0:T(8,128)(2,1)} %all-reduce.10.cloned.1.call-done) | copy-start | bytes 9437188
  400.4 5.3 copy-start.31
  405.7 6.2 copy-start.20
  411.8 155.6 %copy-start.45 = (bf16[8,192]{1,0:T(8,128)(2,1)S(1)}, bf16[8,192]{1,0:T(8,128)(2,1)}, u32[]{:S(2)}) copy-start(bf16[8,192]{1,0:T(8,128)(2,1)} %copy-done.44) | copy-start | bytes 9220
  419.8 4.4 copy-start.22
  424.1 6.7 %copy-start.2 = (f32[3,512,1536]{2,1,0:T(8,128)}, f32[3,512,1536]{2,1,0:T(8,128)S(1)}, u32[]{:S(2)}) copy-start(f32[3,512,1536]{2,1,0:T(8,128)S(1)} %fusion.220) | copy-start | bytes 28311556 | tf_op jit(solution)/shard_map/while
  440.3 5.1 copy-start.3
  440.3 5.3 copy-start.12
  440.3 6.8 %copy-start.23 = (bf16[512,192]{0,1:T(8,128)(2,1)S(1)}, bf16[512,192]{0,1:T(8,128)(2,1)}, u32[]{:S(2)}) copy-start(bf16[512,192]{0,1:T(8,128)(2,1)} %copy-done.22) | copy-start | bytes 589828 | tf_op jit(solution)/shard_map/while
  463.0 6.7 %copy-start.2 = (f32[3,512,1536]{2,1,0:T(8,128)}, f32[3,512,1536]{2,1,0:T(8,128)S(1)}, u32[]{:S(2)}) copy-start(f32[3,512,1536]{2,1,0:T(8,128)S(1)} %fusion.220) | copy-start | bytes 28311556 | tf_op jit(solution)/shard_map/while
  479.1 5.1 copy-start.3
  479.1 5.3 copy-start.12
  479.1 6.8 %copy-start.23 = (bf16[512,192]{0,1:T(8,128)(2,1)S(1)}, bf16[512,192]{0,1:T(8,128)(2,1)}, u32[]{:S(2)}) copy-start(bf16[512,192]{0,1:T(8,128)(2,1)} %copy-done.22) | copy-start | bytes 589828 | tf_op jit(solution)/shard_map/while
  497.5 4.4 copy-start.22
  501.8 6.7 %copy-start.2 = (f32[3,512,1536]{2,1,0:T(8,128)}, f32[3,512,1536]{2,1,0:T(8,128)S(1)}, u32[]{:S(2)}) copy-start(f32[3,512,1536]{2,1,0:T(8,128)S(1)} %fusion.220) | copy-start | bytes 28311556 | tf_op jit(solution)/shard_map/while
  518.0 5.1 copy-start.3
  518.0 5.3 copy-start.12
  518.0 6.8 %copy-start.23 = (bf16[512,192]{0,1:T(8,128)(2,1)S(1)}, bf16[512,192]{0,1:T(8,128)(2,1)}, u32[]{:S(2)}) copy-start(bf16[512,192]{0,1:T(8,128)(2,1)} %copy-done.22) | copy-start | bytes 589828 | tf_op jit(solution)/shard_map/while
  540.7 6.7 %copy-start.2 = (f32[3,512,1536]{2,1,0:T(8,128)}, f32[3,512,1536]{2,1,0:T(8,128)S(1)}, u32[]{:S(2)}) copy-start(f32[3,512,1536]{2,1,0:T(8,128)S(1)} %fusion.220) | copy-start | bytes 28311556 | tf_op jit(solution)/shard_map/while
  556.8 5.1 copy-start.3
  556.8 5.3 copy-start.12
  556.8 6.8 %copy-start.23 = (bf16[512,192]{0,1:T(8,128)(2,1)S(1)}, bf16[512,192]{0,1:T(8,128)(2,1)}, u32[]{:S(2)}) copy-start(bf16[512,192]{0,1:T(8,128)(2,1)} %copy-done.22) | copy-start | bytes 589828 | tf_op jit(solution)/shard_map/while
  569.9 5.9 copy-start.24
  570.1 5.7 copy-start.16
  570.1 5.7 copy-start.35
  576.9 8.7 %copy-start.47 = (u32[32]{0:T(128)S(1)}, u32[32]{0:T(128)}, u32[]{:S(2)}) copy-start(u32[32]{0:T(128)} %constant.162) | copy-start | bytes 388
  576.9 10.0 %copy-start.41 = (f32[768]{0:T(1024)S(1)}, f32[768]{0:T(1024)}, u32[]{:S(2)}) copy-start(f32[768]{0:T(1024)} %param.28) | copy-start | bytes 9220
  576.9 79.5 %copy-start.1 = (bf16[768,768]{1,0:T(8,128)(2,1)S(1)}, bf16[768,768]{1,0:T(8,128)(2,1)}, u32[]{:S(2)}) copy-start(bf16[768,768]{1,0:T(8,128)(2,1)} %param.25) | copy-start | bytes 3538948
  (31 other events, 82.1 us)
Sparse Core Ops, SparseCore 0:
  88.7 84.7 all-gather.2
  211.4 68.4 all-reduce.7
  323.4 68.5 all-reduce.9
  585.0 68.5 all-reduce.11
